TPU v7x, 32 devices: a whole 2x2x4 slice. The times are simulated.
32 devices in a mesh: pb: 4 (over y, core), ka: 8 (over z, x).
Axes of the slice: x: 2, y: 2, z: 4, core: 2. Of those that a mesh axis runs over, the one named last changes fastest.
Arguments:
- queries: float32 [2048, 128], P('pb'), may hold values from -36 to 36
- cache_keys: float32 [65536, 128], P('ka'), may hold values from -4 to 4
- cache_values: float32 [65536, 128], P('ka'), may hold values from -6 to 6
- kept_index: int32 [4096], P('ka'), may hold values from 0 to 65535, as said below
Outputs:
- fitted: float32 [4096, 128], P('ka')
Inputs may be any that keep to these rules, and one draw needn't show every extreme that they name: `kept_index`: Increasing; the t-th kept index lies among the cache rows t * (16) to (t + 1) * 16 - 1, so the kept keys of a device are rows of its own block of the cache.
All inputs are finite; a program needn't handle non-finite values.
Results may differ from a plain program's by a relative error of at most 0.0003.
Values sent between devices are 32-bit elements; how exact they have to be, the bound alone decides.
A program may use at most 128 MiB of HBM per device.

v0:
```python
import math
import jax
import jax.numpy as jnp
from jax import lax
from jax.sharding import PartitionSpec as P

ITERS = 2
ridge_weight = 0.01
highest = lax.Precision.HIGHEST


def contract(left_side, right_side, left_dim, right_dim):
    return lax.dot_general(
        left_side,
        right_side,
        (((left_dim,), (right_dim,)), ((), ())),
        precision=highest,
        preferred_element_type=jnp.float32,
    )


def column_sums(left_side, right_side):
    return jnp.sum(left_side * right_side, axis=0, keepdims=True)


def padded(rows, *tail):
    used = sum((part.shape[0] for part in tail))
    fill = jnp.zeros((-used % 8, rows.shape[1]), rows.dtype)
    return jnp.concatenate((rows,) + tail + (fill,), axis=0)


def shards(queries, cache_keys, cache_values, kept_index):
    query_rows, head_width = queries.shape
    inverse_root = 1.0 / math.sqrt(head_width)
    cache_rows = cache_keys.shape[0]
    block_size = min(1024, cache_rows)
    blocks = cache_rows // block_size
    local_kept = kept_index - lax.axis_index("ka") * cache_rows
    kept_keys = jnp.take(cache_keys, local_kept, axis=0)
    kept_scores = contract(queries, kept_keys, 1, 1) * inverse_root
    kept_top = jnp.max(kept_scores, axis=1)
    kept_exponent = jnp.exp(kept_scores - kept_top[:, None])
    kept_total = jnp.sum(kept_exponent, axis=1)

    def step(block_number, state):
        top, total, numerator = state
        start = block_number * block_size
        keys_block = lax.dynamic_slice_in_dim(cache_keys, start, block_size, axis=0)
        values_block = lax.dynamic_slice_in_dim(cache_values, start, block_size, axis=0)
        scores = contract(queries, keys_block, 1, 1) * inverse_root
        top_next = jnp.maximum(top, jnp.max(scores, axis=1))
        factor = jnp.exp(top - top_next)
        exponent = jnp.exp(scores - top_next[:, None])
        return (
            top_next,
            total * factor + jnp.sum(exponent, axis=1),
            numerator * factor[:, None] + contract(exponent, values_block, 1, 0),
        )

    top, total, numerator = lax.fori_loop(
        0,
        blocks,
        step,
        (
            jnp.full((query_rows,), -jnp.inf, jnp.float32),
            jnp.zeros((query_rows,), jnp.float32),
            jnp.zeros((query_rows, head_width), jnp.float32),
        ),
    )
    stats = jnp.concatenate((top, total, kept_top, kept_total)).reshape(-1, head_width)
    gathered = lax.all_gather(padded(numerator, stats), "ka")
    shares = gathered.shape[0]
    gathered_stats = gathered[:, query_rows : query_rows + stats.shape[0]]
    gathered_stats = gathered_stats.reshape(shares, 4, query_rows)
    factors = jnp.exp(gathered_stats[:, 0] - jnp.max(gathered_stats[:, 0], axis=0))
    target_total = jnp.sum(gathered_stats[:, 1] * factors, axis=0)
    target = jnp.sum(gathered[:, :query_rows] * factors[:, :, None], axis=0)
    target = target / target_total[:, None]
    kept_joint = jnp.max(gathered_stats[:, 2], axis=0)
    joint_total = jnp.sum(gathered_stats[:, 3] * jnp.exp(gathered_stats[:, 2] - kept_joint), axis=0)
    weights = kept_exponent * (jnp.exp(kept_top - kept_joint) / joint_total)[:, None]
    residual = lax.psum(contract(weights, target, 0, 0), "pb")
    kept_rows = residual.shape[0]
    fitted = jnp.zeros_like(residual)
    direction = residual
    updates = None
    norm_now = None
    length_now = None
    for iteration in range(ITERS):
        final_turn = iteration + 1 == ITERS
        forward = contract(weights, residual, 1, 0)
        if iteration == 0:
            summed = lax.psum(padded(forward, column_sums(residual, residual)), "ka")
            updates = summed[:query_rows]
            norm_now = summed[query_rows : query_rows + 1]
            length_now = norm_now
        else:
            summed = lax.psum(
                padded(forward, column_sums(residual, residual), column_sums(residual, direction)),
                "ka",
            )
            norm_next = summed[query_rows : query_rows + 1]
            crossed = summed[query_rows + 1 : query_rows + 2]
            ratio = norm_next / norm_now
            direction = residual + ratio * direction
            updates = summed[:query_rows] + ratio * updates
            length_now = norm_next + 2.0 * ratio * crossed + ratio * ratio * length_now
            norm_now = norm_next
        energy = column_sums(updates, updates)
        if final_turn:
            energy = lax.psum(energy, "pb")
            fitted = fitted + norm_now / (energy + ridge_weight * length_now) * direction
        else:
            summed = lax.psum(padded(contract(weights, updates, 0, 0), energy), "pb")
            operator_image = summed[:kept_rows] + ridge_weight * direction
            energy = summed[kept_rows : kept_rows + 1]
            step_length = norm_now / (energy + ridge_weight * length_now)
            fitted = fitted + step_length * direction
            residual = residual - step_length * operator_image
    return fitted


def solution(mesh):
    in_specs = (P("pb", None), P("ka", None), P("ka", None), P("ka"))
    out_specs = P("ka", None)
    return jax.shard_map(shards, mesh=mesh, in_specs=in_specs, out_specs=out_specs, check_vma=False)
```

profile of v0, /device:TPU:0, one launch (start us, length us, event | category | flops | bytes accessed | tf_op | source)
XLA Modules:
  0.0 368.8 jit_solution(18405595993020933643)
XLA Ops:
  6.5 0.7 compare_and_fusion
  7.3 3.2 gather_fusion
  10.5 64.1 %while.18 = (s32[]{:T(128)}, f32[512]{0:T(512)S(1)}, f32[512]{0:T(512)S(1)}, f32[512,128]{1,0:T(8,128)S(1)}, f32[8192,128]{1,0:T(8,128)}, /*index=5*/f32[512,128...) while((s32[]{:T(128)}, f32[512]{0:T(512)S(1)}, ...), condition=%wide.region_4.5_spmd.clone, body=%wide.region_1.0_spmd.clone.sunk | while | flops 1614481920 | bytes 8159415 | solution.py:60
  10.5 2.9 multiply_reduce_fusion.6
  13.5 0.4 fusion.60
  13.9 4.6 %fusion.62 = f32[512,128]{1,0:T(8,128)S(1)} fusion(f32[1024,512]{1,0:T(8,128)S(1)} %get-tuple-element.239, f32[512]{0:T(512)S(1)} %select_maximum_fusion.2, f32[8192,128]{1,0:T(8,128)} %get-tuple-element.270, s32[]{:T(128)S(6)} %select_n.27, f32[512,128]{1,0:T(8,128)S(1)} %get-tuple-element.256, f32[512]{0:T(512)S(1)} %get-tuple-element.241, ...), kind=kOutput, calls=%fused_computation.5.clone.1 | convolution fusion | flops 806551552 | bytes 3149829 | tf_op jit(solution)/shard_map/while/body/eval_jaxpr/dot_general | solution.py:13
  18.6 2.9 multiply_reduce_fusion.6
  21.5 0.4 fusion.60
  21.9 4.6 %fusion.62 = f32[512,128]{1,0:T(8,128)S(1)} fusion(f32[1024,512]{1,0:T(8,128)S(1)} %get-tuple-element.239, f32[512]{0:T(512)S(1)} %select_maximum_fusion.2, f32[8192,128]{1,0:T(8,128)} %get-tuple-element.270, s32[]{:T(128)S(6)} %select_n.27, f32[512,128]{1,0:T(8,128)S(1)} %get-tuple-element.256, f32[512]{0:T(512)S(1)} %get-tuple-element.241, ...), kind=kOutput, calls=%fused_computation.5.clone.1 | convolution fusion | flops 806551552 | bytes 3149829 | tf_op jit(solution)/shard_map/while/body/eval_jaxpr/dot_general | solution.py:13
  26.6 2.9 multiply_reduce_fusion.6
  29.5 0.4 fusion.60
  29.9 4.6 %fusion.62 = f32[512,128]{1,0:T(8,128)S(1)} fusion(f32[1024,512]{1,0:T(8,128)S(1)} %get-tuple-element.239, f32[512]{0:T(512)S(1)} %select_maximum_fusion.2, f32[8192,128]{1,0:T(8,128)} %get-tuple-element.270, s32[]{:T(128)S(6)} %select_n.27, f32[512,128]{1,0:T(8,128)S(1)} %get-tuple-element.256, f32[512]{0:T(512)S(1)} %get-tuple-element.241, ...), kind=kOutput, calls=%fused_computation.5.clone.1 | convolution fusion | flops 806551552 | bytes 3149829 | tf_op jit(solution)/shard_map/while/body/eval_jaxpr/dot_general | solution.py:13
  34.6 2.9 multiply_reduce_fusion.6
  37.5 0.4 fusion.60
  37.9 4.6 %fusion.62 = f32[512,128]{1,0:T(8,128)S(1)} fusion(f32[1024,512]{1,0:T(8,128)S(1)} %get-tuple-element.239, f32[512]{0:T(512)S(1)} %select_maximum_fusion.2, f32[8192,128]{1,0:T(8,128)} %get-tuple-element.270, s32[]{:T(128)S(6)} %select_n.27, f32[512,128]{1,0:T(8,128)S(1)} %get-tuple-element.256, f32[512]{0:T(512)S(1)} %get-tuple-element.241, ...), kind=kOutput, calls=%fused_computation.5.clone.1 | convolution fusion | flops 806551552 | bytes 3149829 | tf_op jit(solution)/shard_map/while/body/eval_jaxpr/dot_general | solution.py:13
  42.6 2.9 multiply_reduce_fusion.6
  45.5 0.4 fusion.60
  46.0 4.6 %fusion.62 = f32[512,128]{1,0:T(8,128)S(1)} fusion(f32[1024,512]{1,0:T(8,128)S(1)} %get-tuple-element.239, f32[512]{0:T(512)S(1)} %select_maximum_fusion.2, f32[8192,128]{1,0:T(8,128)} %get-tuple-element.270, s32[]{:T(128)S(6)} %select_n.27, f32[512,128]{1,0:T(8,128)S(1)} %get-tuple-element.256, f32[512]{0:T(512)S(1)} %get-tuple-element.241, ...), kind=kOutput, calls=%fused_computation.5.clone.1 | convolution fusion | flops 806551552 | bytes 3149829 | tf_op jit(solution)/shard_map/while/body/eval_jaxpr/dot_general | solution.py:13
  50.6 2.9 multiply_reduce_fusion.6
  53.6 0.4 fusion.60
  54.0 4.6 %fusion.62 = f32[512,128]{1,0:T(8,128)S(1)} fusion(f32[1024,512]{1,0:T(8,128)S(1)} %get-tuple-element.239, f32[512]{0:T(512)S(1)} %select_maximum_fusion.2, f32[8192,128]{1,0:T(8,128)} %get-tuple-element.270, s32[]{:T(128)S(6)} %select_n.27, f32[512,128]{1,0:T(8,128)S(1)} %get-tuple-element.256, f32[512]{0:T(512)S(1)} %get-tuple-element.241, ...), kind=kOutput, calls=%fused_computation.5.clone.1 | convolution fusion | flops 806551552 | bytes 3149829 | tf_op jit(solution)/shard_map/while/body/eval_jaxpr/dot_general | solution.py:13
  58.6 2.9 multiply_reduce_fusion.6
  61.6 0.4 fusion.60
  62.0 4.6 %fusion.62 = f32[512,128]{1,0:T(8,128)S(1)} fusion(f32[1024,512]{1,0:T(8,128)S(1)} %get-tuple-element.239, f32[512]{0:T(512)S(1)} %select_maximum_fusion.2, f32[8192,128]{1,0:T(8,128)} %get-tuple-element.270, s32[]{:T(128)S(6)} %select_n.27, f32[512,128]{1,0:T(8,128)S(1)} %get-tuple-element.256, f32[512]{0:T(512)S(1)} %get-tuple-element.241, ...), kind=kOutput, calls=%fused_computation.5.clone.1 | convolution fusion | flops 806551552 | bytes 3149829 | tf_op jit(solution)/shard_map/while/body/eval_jaxpr/dot_general | solution.py:13
  66.7 2.9 multiply_reduce_fusion.6
  69.6 0.4 fusion.60
  70.0 4.6 %fusion.62 = f32[512,128]{1,0:T(8,128)S(1)} fusion(f32[1024,512]{1,0:T(8,128)S(1)} %get-tuple-element.239, f32[512]{0:T(512)S(1)} %select_maximum_fusion.2, f32[8192,128]{1,0:T(8,128)} %get-tuple-element.270, s32[]{:T(128)S(6)} %select_n.27, f32[512,128]{1,0:T(8,128)S(1)} %get-tuple-element.256, f32[512]{0:T(512)S(1)} %get-tuple-element.241, ...), kind=kOutput, calls=%fused_computation.5.clone.1 | convolution fusion | flops 806551552 | bytes 3149829 | tf_op jit(solution)/shard_map/while/body/eval_jaxpr/dot_general | solution.py:13
  74.7 1.1 fusion.49
  75.7 0.2 fusion.14
  75.9 1.9 concatenate.27
  77.8 0.0 all-gather.3.cloned.1.call-update
  77.9 0.0 all-reduce.5.cloned.1.call-start
  77.9 52.8 %all-gather.3.cloned.1.call-done = f32[4224,128]{1,0:T(8,128)} async-done(((f32[528,128]{1,0:T(8,128)}), f32[4224,128]{1,0:T(8,128)}) %all-gather.3.cloned.1.call-update) | async-done | bytes 2162704 | tf_op jit(solution)/shard_map/all_gather | solution.py:71
  130.7 0.8 slice.56
  131.6 0.1 slice_reduce_fusion
  131.7 1.9 fusion.12
  133.6 1.8 fusion.21
  135.4 0.0 all-reduce.5.cloned.1.call-update
  135.5 0.0 all-reduce.7.cloned.1.call-start
  135.5 0.1 pad.9.clone
  135.6 30.5 %all-reduce.5.cloned.1.call-done = f32[512,128]{1,0:T(8,128)} async-done(((f32[512,128]{1,0:T(8,128)}), f32[512,128]{1,0:T(8,128)}) %all-reduce.5.cloned.1.call-update) | async-done | bytes 262160 | tf_op jit(solution)/shard_map/psum | solution.py:82
  166.1 1.0 multiply_reduce_fusion.4
  167.1 2.8 fusion.19
  169.9 0.8 maximum_maximum_fusion
  170.7 0.0 all-reduce.7.cloned.1.call-update
  170.8 0.0 all-reduce.9.cloned.1.call-start
  170.8 70.6 %all-reduce.7.cloned.1.call-done = f32[520,128]{1,0:T(8,128)} async-done(((f32[520,128]{1,0:T(8,128)}), f32[520,128]{1,0:T(8,128)}) %all-reduce.7.cloned.1.call-update) | async-done | bytes 266256 | tf_op jit(solution)/shard_map/psum | solution.py:93
  241.5 1.1 multiply_reduce_fusion.3
  242.6 2.0 fusion.17
  244.6 0.8 maximum_maximum_fusion.1
  245.4 0.0 all-reduce.9.cloned.1.call-update
  245.4 0.2 all-reduce.11.cloned.1.call-start
  245.6 0.1 pad.3.clone
  245.7 30.5 %all-reduce.9.cloned.1.call-done = f32[520,128]{1,0:T(8,128)} async-done(((f32[520,128]{1,0:T(8,128)}), f32[520,128]{1,0:T(8,128)}) %all-reduce.9.cloned.1.call-update) | async-done | bytes 266256 | tf_op jit(solution)/shard_map/psum | solution.py:114
  276.2 0.8 fusion.44
  276.9 2.8 fusion.15
  279.7 1.0 multiply_reduce_fusion.2
  280.8 0.8 maximum_maximum_fusion.2
  281.6 71.7 %all-reduce.11.cloned.1.call-done = f32[520,128]{1,0:T(8,128)} async-done(((f32[520,128]{1,0:T(8,128)}), f32[520,128]{1,0:T(8,128)}) %all-reduce.11.cloned.1.call-update) | async-done | bytes 266256 | tf_op jit(solution)/shard_map/psum | solution.py:98
  353.3 0.7 slice_divide_fusion
  354.0 1.0 fusion.24
  355.0 5.7 %psum.39 = f32[1,128]{1,0:T(1,128)S(1)} all-reduce(f32[1,128]{1,0:T(1,128)S(1)} %bitcast.57), channel_id=1, replica_groups=mesh['pb'=4,'ka'=8] {'pb'}, use_global_device_ids=true, to_apply=%region_20.21 | all-reduce | flops 128 | bytes 1024 | tf_op jit(solution)/shard_map/psum | solution.py:111
  360.7 0.8 fusion.45
  361.4 0.8 multiply_add_fusion
  (43 shorter events, 0.3 us)
Async XLA Ops:
  6.5 4.0 %copy-start = (f32[512,128]{1,0:T(8,128)S(1)}, f32[512,128]{1,0:T(8,128)}, u32[]{:S(2)}) copy-start(f32[512,128]{1,0:T(8,128)} %param.6) | copy-start | bytes 786436
  6.5 124.1 %all-gather.3.cloned.1.call-start = ((), (), s32[]{:S(2)}) async-start(), calls=%async_computation.4 | async-start | bytes 2433024 | tf_op jit(solution)/shard_map/all_gather | solution.py:71
  77.9 88.2 %all-reduce.5.cloned.1.call-start = ((), (), s32[]{:S(2)}) async-start(), calls=%async_computation | async-start | bytes 524288 | tf_op jit(solution)/shard_map/psum | solution.py:82
  135.5 106.0 %all-reduce.7.cloned.1.call-start = ((), (), s32[]{:S(2)}) async-start(), calls=%async_computation.1 | async-start | bytes 532480 | tf_op jit(solution)/shard_map/psum | solution.py:93
  169.9 107.0 %copy-start.1 = (f32[512,128]{1,0:T(8,128)S(1)}, f32[512,128]{1,0:T(8,128)}, u32[]{:S(2)}) copy-start(f32[512,128]{1,0:T(8,128)} %all-reduce.5.cloned.1.call-done) | copy-start | bytes 786436
  170.8 105.4 %all-reduce.9.cloned.1.call-start = ((), (), s32[]{:S(2)}) async-start(), calls=%async_computation.2 | async-start | bytes 532480 | tf_op jit(solution)/shard_map/psum | solution.py:114
  241.5 34.7 %copy-start.2 = (f32[520,128]{1,0:T(8,128)S(1)}, f32[520,128]{1,0:T(8,128)}, u32[]{:S(2)}) copy-start(f32[520,128]{1,0:T(8,128)} %all-reduce.7.cloned.1.call-done) | copy-start | bytes 798724
  245.4 107.9 %all-reduce.11.cloned.1.call-start = ((), (), s32[]{:S(2)}) async-start(), calls=%async_computation.3 | async-start | bytes 532480 | tf_op jit(solution)/shard_map/psum | solution.py:98
  276.2 85.3 %copy-start.3 = (f32[520,128]{1,0:T(8,128)S(1)}, f32[520,128]{1,0:T(8,128)}, u32[]{:S(2)}) copy-start(f32[520,128]{1,0:T(8,128)} %all-reduce.9.cloned.1.call-done) | copy-start | bytes 798724
Sparse Core Ops, SparseCore 0:
  78.0 52.6 all-gather.2
  135.6 30.4 all-reduce.4
  170.9 70.5 all-reduce.6
  245.5 30.6 all-reduce.8
  281.7 71.5 all-reduce.10
where the time goes:
time: 370 us; the launch traced here: 369 us
  waiting for transfers between devices  256 us (69%)
  matrix products  70.8 us (19%)
  other arithmetic  16.1 us (4%)
  between operations  13.2 us (4%)
  local copies, waits for them, and re-layouts  6.21 us (2%)
  blocking collectives  5.66 us (2%)
    psum x1, waiting for transfers between devices, shards(): lax.psum(padded(forward, column_sums(residual, residual), column_sums(res...  71.7 us
    dot_general x21, matrix products, contract(): lax.dot_general(left_side, right_side, (((left_dim,), (right_dim,)), ((),...  70.8 us
    psum x1, waiting for transfers between devices, shards(): summed = lax.psum(padded(forward, column_sums(residual, residual)), 'ka')  70.6 us
    all_gather x1, waiting for transfers between devices, shards(): gathered = lax.all_gather(padded(numerator, stats), 'ka')  52.8 us
    psum x1, waiting for transfers between devices, shards(): residual = lax.psum(contract(weights, target, 0, 0), 'pb')  30.5 us
    psum x1, waiting for transfers between devices, shards(): summed = lax.psum(padded(contract(weights, updates, 0, 0), energy), 'pb')  30.5 us
  transfers between devices with their start and end apart: 5, of which 5 were waited for; matrix products, arithmetic and copies ran while one was open for 0% of the time, Pallas kernels for 0%

commit v1 on v0

--- a/solution.py
+++ b/solution.py
@@ -3,6 +3,7 @@
 import jax.numpy as jnp
 from jax import lax
 from jax.sharding import PartitionSpec as P
+from jax.lax import all_gather
 
 ITERS = 2
 ridge_weight = 0.01
@@ -79,7 +80,8 @@
     kept_joint = jnp.max(gathered_stats[:, 2], axis=0)
     joint_total = jnp.sum(gathered_stats[:, 3] * jnp.exp(gathered_stats[:, 2] - kept_joint), axis=0)
     weights = kept_exponent * (jnp.exp(kept_top - kept_joint) / joint_total)[:, None]
-    residual = lax.psum(contract(weights, target, 0, 0), "pb")
+    spots_compute = lambda array_here: jnp.sum(all_gather(array_here, axis_name="pb"), axis=0)
+    residual = spots_compute(contract(weights, target, 0, 0))
     kept_rows = residual.shape[0]
     fitted = jnp.zeros_like(residual)
     direction = residual

time: 370 us -> 354 us (0.957)
  waiting for transfers between devices: 256 us -> 241 us
    psum x1 -> x0, waiting for transfers between devices: 30.5 us -> none  [shards(): residual = lax.psum(contract(weights, target, 0, 0), 'pb')]
    all_gather x0 -> x1, waiting for transfers between devices: none -> 15.3 us  [shards(): all_gather(array_here, axis_name='pb')]
where the time goes in v1:
time: 354 us; the launch traced here: 353 us
  waiting for transfers between devices  241 us (68%)
  matrix products  69.8 us (20%)
  other arithmetic  16.4 us (5%)
  between operations  13.2 us (4%)
  local copies, waits for them, and re-layouts  6.21 us (2%)
  blocking collectives  5.66 us (2%)
    psum x1, waiting for transfers between devices, shards(): lax.psum(padded(forward, column_sums(residual, residual), column_sums(res...  71.6 us
    psum x1, waiting for transfers between devices, shards(): summed = lax.psum(padded(forward, column_sums(residual, residual)), 'ka')  70.7 us
    dot_general x21, matrix products, contract(): lax.dot_general(left_side, right_side, (((left_dim,), (right_dim,)), ((),...  69.8 us
    all_gather x1, waiting for transfers between devices, shards(): gathered = lax.all_gather(padded(numerator, stats), 'ka')  52.8 us
    psum x1, waiting for transfers between devices, shards(): summed = lax.psum(padded(contract(weights, updates, 0, 0), energy), 'pb')  30.4 us
    all_gather x1, waiting for transfers between devices, shards(): all_gather(array_here, axis_name='pb')  15.3 us
  transfers between devices with their start and end apart: 5, of which 5 were waited for; matrix products, arithmetic and copies ran while one was open for 0% of the time, Pallas kernels for 0%

profile of v1, /device:TPU:0, one launch (start us, length us, event | category | flops | bytes accessed | tf_op | source)
XLA Modules:
  0.0 352.9 jit_solution(11141588093737930138)
XLA Ops:
  6.5 0.7 compare_and_fusion
  7.3 3.2 gather_fusion
  10.5 64.1 %while.18 = (s32[]{:T(128)}, f32[512]{0:T(512)S(1)}, f32[512]{0:T(512)S(1)}, f32[512,128]{1,0:T(8,128)S(1)}, f32[8192,128]{1,0:T(8,128)}, /*index=5*/f32[512,128...) while((s32[]{:T(128)}, f32[512]{0:T(512)S(1)}, ...), condition=%wide.region_4.5_spmd.clone, body=%wide.region_1.0_spmd.clone.sunk | while | flops 1614481920 | bytes 8159415 | solution.py:61
  10.5 2.9 multiply_reduce_fusion.6
  13.5 0.4 fusion.60
  13.9 4.6 %fusion.62 = f32[512,128]{1,0:T(8,128)S(1)} fusion(f32[1024,512]{1,0:T(8,128)S(1)} %get-tuple-element.239, f32[512]{0:T(512)S(1)} %select_maximum_fusion.2, f32[8192,128]{1,0:T(8,128)} %get-tuple-element.270, s32[]{:T(128)S(6)} %select_n.27, f32[512,128]{1,0:T(8,128)S(1)} %get-tuple-element.256, f32[512]{0:T(512)S(1)} %get-tuple-element.241, ...), kind=kOutput, calls=%fused_computation.5.clone.1 | convolution fusion | flops 806551552 | bytes 3149829 | tf_op jit(solution)/shard_map/while/body/eval_jaxpr/dot_general | solution.py:14
  18.6 2.9 multiply_reduce_fusion.6
  21.5 0.4 fusion.60
  21.9 4.6 %fusion.62 = f32[512,128]{1,0:T(8,128)S(1)} fusion(f32[1024,512]{1,0:T(8,128)S(1)} %get-tuple-element.239, f32[512]{0:T(512)S(1)} %select_maximum_fusion.2, f32[8192,128]{1,0:T(8,128)} %get-tuple-element.270, s32[]{:T(128)S(6)} %select_n.27, f32[512,128]{1,0:T(8,128)S(1)} %get-tuple-element.256, f32[512]{0:T(512)S(1)} %get-tuple-element.241, ...), kind=kOutput, calls=%fused_computation.5.clone.1 | convolution fusion | flops 806551552 | bytes 3149829 | tf_op jit(solution)/shard_map/while/body/eval_jaxpr/dot_general | solution.py:14
  26.6 2.9 multiply_reduce_fusion.6
  29.5 0.4 fusion.60
  29.9 4.6 %fusion.62 = f32[512,128]{1,0:T(8,128)S(1)} fusion(f32[1024,512]{1,0:T(8,128)S(1)} %get-tuple-element.239, f32[512]{0:T(512)S(1)} %select_maximum_fusion.2, f32[8192,128]{1,0:T(8,128)} %get-tuple-element.270, s32[]{:T(128)S(6)} %select_n.27, f32[512,128]{1,0:T(8,128)S(1)} %get-tuple-element.256, f32[512]{0:T(512)S(1)} %get-tuple-element.241, ...), kind=kOutput, calls=%fused_computation.5.clone.1 | convolution fusion | flops 806551552 | bytes 3149829 | tf_op jit(solution)/shard_map/while/body/eval_jaxpr/dot_general | solution.py:14
  34.6 2.9 multiply_reduce_fusion.6
  37.5 0.4 fusion.60
  37.9 4.6 %fusion.62 = f32[512,128]{1,0:T(8,128)S(1)} fusion(f32[1024,512]{1,0:T(8,128)S(1)} %get-tuple-element.239, f32[512]{0:T(512)S(1)} %select_maximum_fusion.2, f32[8192,128]{1,0:T(8,128)} %get-tuple-element.270, s32[]{:T(128)S(6)} %select_n.27, f32[512,128]{1,0:T(8,128)S(1)} %get-tuple-element.256, f32[512]{0:T(512)S(1)} %get-tuple-element.241, ...), kind=kOutput, calls=%fused_computation.5.clone.1 | convolution fusion | flops 806551552 | bytes 3149829 | tf_op jit(solution)/shard_map/while/body/eval_jaxpr/dot_general | solution.py:14
  42.6 2.9 multiply_reduce_fusion.6
  45.5 0.4 fusion.60
  46.0 4.6 %fusion.62 = f32[512,128]{1,0:T(8,128)S(1)} fusion(f32[1024,512]{1,0:T(8,128)S(1)} %get-tuple-element.239, f32[512]{0:T(512)S(1)} %select_maximum_fusion.2, f32[8192,128]{1,0:T(8,128)} %get-tuple-element.270, s32[]{:T(128)S(6)} %select_n.27, f32[512,128]{1,0:T(8,128)S(1)} %get-tuple-element.256, f32[512]{0:T(512)S(1)} %get-tuple-element.241, ...), kind=kOutput, calls=%fused_computation.5.clone.1 | convolution fusion | flops 806551552 | bytes 3149829 | tf_op jit(solution)/shard_map/while/body/eval_jaxpr/dot_general | solution.py:14
  50.6 2.9 multiply_reduce_fusion.6
  53.6 0.4 fusion.60
  54.0 4.6 %fusion.62 = f32[512,128]{1,0:T(8,128)S(1)} fusion(f32[1024,512]{1,0:T(8,128)S(1)} %get-tuple-element.239, f32[512]{0:T(512)S(1)} %select_maximum_fusion.2, f32[8192,128]{1,0:T(8,128)} %get-tuple-element.270, s32[]{:T(128)S(6)} %select_n.27, f32[512,128]{1,0:T(8,128)S(1)} %get-tuple-element.256, f32[512]{0:T(512)S(1)} %get-tuple-element.241, ...), kind=kOutput, calls=%fused_computation.5.clone.1 | convolution fusion | flops 806551552 | bytes 3149829 | tf_op jit(solution)/shard_map/while/body/eval_jaxpr/dot_general | solution.py:14
  58.6 2.9 multiply_reduce_fusion.6
  61.6 0.4 fusion.60
  62.0 4.6 %fusion.62 = f32[512,128]{1,0:T(8,128)S(1)} fusion(f32[1024,512]{1,0:T(8,128)S(1)} %get-tuple-element.239, f32[512]{0:T(512)S(1)} %select_maximum_fusion.2, f32[8192,128]{1,0:T(8,128)} %get-tuple-element.270, s32[]{:T(128)S(6)} %select_n.27, f32[512,128]{1,0:T(8,128)S(1)} %get-tuple-element.256, f32[512]{0:T(512)S(1)} %get-tuple-element.241, ...), kind=kOutput, calls=%fused_computation.5.clone.1 | convolution fusion | flops 806551552 | bytes 3149829 | tf_op jit(solution)/shard_map/while/body/eval_jaxpr/dot_general | solution.py:14
  66.7 2.9 multiply_reduce_fusion.6
  69.6 0.4 fusion.60
  70.0 4.6 %fusion.62 = f32[512,128]{1,0:T(8,128)S(1)} fusion(f32[1024,512]{1,0:T(8,128)S(1)} %get-tuple-element.239, f32[512]{0:T(512)S(1)} %select_maximum_fusion.2, f32[8192,128]{1,0:T(8,128)} %get-tuple-element.270, s32[]{:T(128)S(6)} %select_n.27, f32[512,128]{1,0:T(8,128)S(1)} %get-tuple-element.256, f32[512]{0:T(512)S(1)} %get-tuple-element.241, ...), kind=kOutput, calls=%fused_computation.5.clone.1 | convolution fusion | flops 806551552 | bytes 3149829 | tf_op jit(solution)/shard_map/while/body/eval_jaxpr/dot_general | solution.py:14
  74.7 1.1 fusion.49
  75.7 0.2 fusion.14
  75.9 1.9 concatenate.27
  77.8 0.0 all-gather.5.cloned.1.call-update
  77.9 0.0 all-gather.7.cloned.1.call-start
  77.9 52.8 %all-gather.5.cloned.1.call-done = f32[4224,128]{1,0:T(8,128)} async-done(((f32[528,128]{1,0:T(8,128)}), f32[4224,128]{1,0:T(8,128)}) %all-gather.5.cloned.1.call-update) | async-done | bytes 2162704 | tf_op jit(solution)/shard_map/all_gather | solution.py:72
  130.7 0.8 slice.56
  131.6 0.1 slice_reduce_fusion
  131.7 1.9 fusion.12
  133.6 1.8 fusion.21
  135.4 0.0 all-gather.7.cloned.1.call-update
  135.5 0.0 all-reduce.4.cloned.1.call-start
  135.5 0.1 pad.9.clone
  135.6 15.3 %all-gather.7.cloned.1.call-done = f32[2048,128]{1,0:T(8,128)} async-done(((f32[512,128]{1,0:T(8,128)}), f32[2048,128]{1,0:T(8,128)}) %all-gather.7.cloned.1.call-update) | async-done | bytes 1048592 | tf_op jit(solution)/shard_map/all_gather | solution.py:83
  150.8 1.3 reduce_sum.107
  152.2 0.1 multiply_reduce_fusion.4
  152.2 1.8 fusion.19
  154.1 0.8 maximum_maximum_fusion
  154.9 0.0 all-reduce.4.cloned.1.call-update
  154.9 0.0 all-reduce.6.cloned.1.call-start
  155.0 70.7 %all-reduce.4.cloned.1.call-done = f32[520,128]{1,0:T(8,128)} async-done(((f32[520,128]{1,0:T(8,128)}), f32[520,128]{1,0:T(8,128)}) %all-reduce.4.cloned.1.call-update) | async-done | bytes 266256 | tf_op jit(solution)/shard_map/psum | solution.py:95
  225.7 1.1 multiply_reduce_fusion.3
  226.8 2.0 fusion.17
  228.8 0.8 maximum_maximum_fusion.1
  229.6 0.2 all-reduce.8.cloned.1.call-start
  229.8 0.1 pad.3.clone
  229.9 30.4 %all-reduce.6.cloned.1.call-done = f32[520,128]{1,0:T(8,128)} async-done(((f32[520,128]{1,0:T(8,128)}), f32[520,128]{1,0:T(8,128)}) %all-reduce.6.cloned.1.call-update) | async-done | bytes 266256 | tf_op jit(solution)/shard_map/psum | solution.py:116
  260.4 0.8 fusion.44
  261.1 2.8 fusion.15
  263.9 1.0 multiply_reduce_fusion.2
  265.0 0.8 maximum_maximum_fusion.2
  265.8 71.6 %all-reduce.8.cloned.1.call-done = f32[520,128]{1,0:T(8,128)} async-done(((f32[520,128]{1,0:T(8,128)}), f32[520,128]{1,0:T(8,128)}) %all-reduce.8.cloned.1.call-update) | async-done | bytes 266256 | tf_op jit(solution)/shard_map/psum | solution.py:100
  337.4 0.7 slice_divide_fusion
  338.1 1.0 fusion.24
  339.1 5.7 %psum.31 = f32[1,128]{1,0:T(1,128)S(1)} all-reduce(f32[1,128]{1,0:T(1,128)S(1)} %bitcast.59), channel_id=1, replica_groups=mesh['pb'=4,'ka'=8] {'pb'}, use_global_device_ids=true, to_apply=%region_20.21 | all-reduce | flops 128 | bytes 1024 | tf_op jit(solution)/shard_map/psum | solution.py:113
  344.8 0.8 fusion.45
  345.6 0.8 multiply_add_fusion
  (42 shorter events, 0.3 us)
Async XLA Ops:
  6.5 4.0 %copy-start = (f32[512,128]{1,0:T(8,128)S(1)}, f32[512,128]{1,0:T(8,128)}, u32[]{:S(2)}) copy-start(f32[512,128]{1,0:T(8,128)} %param.6) | copy-start | bytes 786436
  6.5 124.1 %all-gather.5.cloned.1.call-start = ((), (), s32[]{:S(2)}) async-start(), calls=%async_computation.3 | async-start | bytes 2433024 | tf_op jit(solution)/shard_map/all_gather | solution.py:72
  77.9 73.0 %all-gather.7.cloned.1.call-start = ((), (), s32[]{:S(2)}) async-start(), calls=%async_computation.4 | async-start | bytes 1310720 | tf_op jit(solution)/shard_map/all_gather | solution.py:83
  135.5 90.2 %all-reduce.4.cloned.1.call-start = ((), (), s32[]{:S(2)}) async-start(), calls=%async_computation | async-start | bytes 532480 | tf_op jit(solution)/shard_map/psum | solution.py:95
  154.9 105.4 %all-reduce.6.cloned.1.call-start = ((), (), s32[]{:S(2)}) async-start(), calls=%async_computation.1 | async-start | bytes 532480 | tf_op jit(solution)/shard_map/psum | solution.py:116
  225.7 34.7 %copy-start.1 = (f32[520,128]{1,0:T(8,128)S(1)}, f32[520,128]{1,0:T(8,128)}, u32[]{:S(2)}) copy-start(f32[520,128]{1,0:T(8,128)} %all-reduce.4.cloned.1.call-done) | copy-start | bytes 798724
  229.6 107.8 %all-reduce.8.cloned.1.call-start = ((), (), s32[]{:S(2)}) async-start(), calls=%async_computation.2 | async-start | bytes 532480 | tf_op jit(solution)/shard_map/psum | solution.py:100
  260.4 85.2 %copy-start.2 = (f32[520,128]{1,0:T(8,128)S(1)}, f32[520,128]{1,0:T(8,128)}, u32[]{:S(2)}) copy-start(f32[520,128]{1,0:T(8,128)} %all-reduce.6.cloned.1.call-done) | copy-start | bytes 798724
Sparse Core Ops, SparseCore 0:
  78.0 52.6 all-gather.4
  135.6 15.2 all-gather.6
  155.0 70.5 all-reduce.3
  229.7 30.5 all-reduce.5
  265.9 71.4 all-reduce.7
